TPU v7x, 32 devices: a whole 2x2x4 slice. The times are simulated.
32 devices in a mesh: depth: 2 (over y), row: 4 (over x, core), col: 4 (over z).
Axes of the slice: x: 2, y: 2, z: 4, core: 2. Of those that a mesh axis runs over, the one named last changes fastest.
Arguments:
- volume: float32 [2, 1024, 1024], P('depth', 'row', 'col'), may hold values from -6 to 6
- psf_spec: float32 [2, 2, 1024, 1024], P(None, 'depth', 'row', 'col'), may hold values from -1.5 to 1.5
- measured: float32 [1024, 1024], P('row', 'col'), may hold values from -6 to 6
- dual: float32 [3, 2, 1024, 1024], P(None, 'depth', 'row', 'col'), may hold values from -3 to 3
Outputs:
- updated: float32 [2, 1024, 1024], P('depth', 'row', 'col')
- shrunk: float32 [3, 2, 1024, 1024], P(None, 'depth', 'row', 'col')
- dual_next: float32 [3, 2, 1024, 1024], P(None, 'depth', 'row', 'col')
All inputs are finite; a program needn't handle non-finite values.
Results may differ from a plain program's by a relative error of at most 0.00005.
Values sent between devices are 32-bit elements; how exact they have to be, the bound alone decides.
A program may use at most 64 MiB of HBM per device.

v0:
```python
import math
import jax
import jax.numpy as jnp
from jax import lax
from jax.sharding import PartitionSpec as P

step_size = 1.0
shrink_level = 0.5
highest = lax.Precision.HIGHEST


def shifted(array, axis, by):
    length = lax.axis_size(axis)
    pairs = [(i, i + by) for i in range(length) if 0 <= i + by < length]
    return lax.ppermute(array, axis, pairs)


def twiddle(first_index, second_index, length, orient):
    phases = first_index[:, None] * second_index[None, :] % length
    angles = phases.astype(jnp.float32) * (orient * 2.0 * math.pi / length)
    return (jnp.cos(angles), jnp.sin(angles))


def complex_mix(field, apply_cos, apply_sin, keep):
    if field.shape[0] == 1:
        real_part = apply_cos(field[0])
        imag_part = apply_sin(field[0])
        return jnp.stack([real_part, imag_part])
    real_part = apply_cos(field[0]) - apply_sin(field[1])
    if keep == 1:
        return real_part[None]
    imag_part = apply_sin(field[0]) + apply_cos(field[1])
    return jnp.stack([real_part, imag_part])


def right_mult(field, cosines, sine_part, keep):

    def apply_cos(part):
        return jnp.dot(part, cosines, precision=highest, preferred_element_type=jnp.float32)

    def apply_sin(part):
        return jnp.dot(part, sine_part, precision=highest, preferred_element_type=jnp.float32)

    return complex_mix(field, apply_cos, apply_sin, keep)


def left_mult(cosines, sine_part, field, keep):

    def apply_cos(part):
        return jnp.einsum(
            "kh,phw->pkw", cosines, part, precision=highest, preferred_element_type=jnp.float32
        )

    def apply_sin(part):
        return jnp.einsum(
            "kh,phw->pkw", sine_part, part, precision=highest, preferred_element_type=jnp.float32
        )

    return complex_mix(field, apply_cos, apply_sin, keep)


def out_parts(field, keep):
    if field.shape[0] == 1:
        return 2
    return keep


def along_columns(field, orient, factor, keep):
    col_block = field.shape[3]
    width_all = col_block * lax.axis_size("col")
    parts_out = out_parts(field, keep)
    targets = lax.axis_index("col") * col_block + jnp.arange(col_block, dtype=jnp.int32)

    def accumulate(running, portion, offset):
        sources = jnp.arange(portion.shape[3], dtype=jnp.int32)
        cosines, sine_part = twiddle(sources, targets, width_all, orient)
        return right_mult(portion, cosines, sine_part, keep)

    start_value = jnp.zeros((parts_out,) + field.shape[1:], jnp.float32)
    result = (
        accumulate(start_value, lax.all_gather(field, "col", axis=3, tiled=True), jnp.int32(0))
        * factor
    )
    return result


def along_rows(field, orient, factor, keep):
    row_block = field.shape[2]
    height_all = row_block * lax.axis_size("row")
    parts_out = out_parts(field, keep)
    targets = lax.axis_index("row") * row_block + jnp.arange(row_block, dtype=jnp.int32)

    def accumulate(running, portion, offset):
        sources = jnp.arange(portion.shape[2], dtype=jnp.int32)
        cosines, sine_part = twiddle(targets, sources, height_all, orient)
        return left_mult(cosines, sine_part, portion, keep)

    start_value = jnp.zeros((parts_out,) + field.shape[1:], jnp.float32)
    result = (
        accumulate(start_value, lax.all_gather(field, "row", axis=2, tiled=True), jnp.int32(0))
        * factor
    )
    return result


def shards(volume, psf_spec, measured, dual):
    planes, row_block, col_block = volume.shape
    height_all = row_block * lax.axis_size("row")
    width_all = col_block * lax.axis_size("col")
    spectra = along_rows(along_columns(volume[None], -1.0, 1.0, 2), -1.0, 1.0, 2)
    kernel_real = psf_spec[0]
    kernel_imag = psf_spec[1]
    prod_real = jnp.sum(kernel_real * spectra[0] - kernel_imag * spectra[1], axis=0, keepdims=True)
    prod_imag = jnp.sum(kernel_real * spectra[1] + kernel_imag * spectra[0], axis=0, keepdims=True)
    local_sum = jnp.stack([prod_real, prod_imag])
    row_global = lax.axis_index("row") * row_block + jnp.arange(row_block, dtype=jnp.int32)
    col_global = lax.axis_index("col") * col_block + jnp.arange(col_block, dtype=jnp.int32)
    inside = ((row_global >= height_all // 4) & (row_global < 3 * height_all // 4))[:, None] & (
        (col_global >= width_all // 4) & (col_global < 3 * width_all // 4)
    )[None, :]
    empty_part = jnp.zeros_like(measured)
    summed_image = lax.psum(local_sum, "depth")
    sensor_image = along_columns(
        along_rows(summed_image, 1.0, 1.0 / height_all, 2), 1.0, 1.0 / width_all, 1
    )[0, 0]
    residual_map = jnp.where(inside, sensor_image - measured, empty_part)
    residual_spec = along_rows(along_columns(residual_map[None, None], -1.0, 1.0, 2), -1.0, 1.0, 2)
    back_real = kernel_real * residual_spec[0] + kernel_imag * residual_spec[1]
    back_imag = kernel_real * residual_spec[1] - kernel_imag * residual_spec[0]
    adjoint = along_columns(
        along_rows(jnp.stack([back_real, back_imag]), 1.0, 1.0 / height_all, 2),
        1.0,
        1.0 / width_all,
        1,
    )[0]
    updated = volume - step_size * adjoint
    plane_ahead = shifted(updated, "depth", -1)
    depth_count = planes * lax.axis_size("depth")
    plane_global = lax.axis_index("depth") * planes + jnp.arange(planes, dtype=jnp.int32)
    diff_depth = jnp.where(
        (plane_global < depth_count - 1)[:, None, None],
        jnp.concatenate([updated[1:], plane_ahead], axis=0) - updated,
        0.0,
    )
    row_ahead = shifted(updated[:, :1, :], "row", -1)
    diff_rows = jnp.where(
        (row_global < height_all - 1)[None, :, None],
        jnp.concatenate([updated[:, 1:, :], row_ahead], axis=1) - updated,
        0.0,
    )
    col_ahead = shifted(updated[:, :, :1], "col", -1)
    diff_cols = jnp.where(
        (col_global < width_all - 1)[None, None, :],
        jnp.concatenate([updated[:, :, 1:], col_ahead], axis=2) - updated,
        0.0,
    )
    combined = jnp.stack([diff_depth, diff_rows, diff_cols]) + dual
    dual_next = jnp.clip(combined, -shrink_level, shrink_level)
    return (updated, combined - dual_next, dual_next)


def solution(mesh):
    placed = (
        P("depth", "row", "col"),
        P(None, "depth", "row", "col"),
        P("row", "col"),
        P(None, "depth", "row", "col"),
    )
    return jax.shard_map(
        shards,
        mesh=mesh,
        in_specs=placed,
        out_specs=(
            P("depth", "row", "col"),
            P(None, "depth", "row", "col"),
            P(None, "depth", "row", "col"),
        ),
        check_vma=False,
    )
```

profile of v0, /device:TPU:0, one launch (start us, length us, event | category | flops | bytes accessed | tf_op | source)
XLA Modules:
  0.0 439.6 jit_solution(15999376654098091278)
XLA Ops:
  8.0 32.3 %all-gather.23.cloned.1.call-done = f32[1,256,1024]{2,1,0:T(8,128)} async-done(((f32[1,256,256]{2,1,0:T(8,128)}), f32[1,256,1024]{2,1,0:T(8,128)}) %all-gather.23.cloned.1.call-update) | async-done | bytes 1048592 | tf_op jit(solution)/shard_map/all_gather | solution.py:81
  40.3 6.9 %convolution_bitcast_fusion.2 = f32[1,1,256,256]{2,3,1,0:T(8,128)S(1)} fusion(f32[1,256,1024]{2,1,0:T(8,128)} %all-gather.23.cloned.1.call-done, s32[256]{0:T(256)S(1)} %iota_add_fusion), kind=kOutput, calls=%fused_computation.31 | convolution fusion | flops 808976384 | bytes 1311744 | tf_op jit(solution)/shard_map/dot_general | solution.py:42
  47.2 5.6 %convolution_bitcast_fusion.3 = f32[1,1,256,256]{2,3,1,0:T(8,128)S(1)} fusion(f32[1,256,1024]{2,1,0:T(8,128)S(1)} %copy-done.10, s32[256]{0:T(256)S(1)} %iota_add_fusion), kind=kOutput, calls=%fused_computation.32 | convolution fusion | flops 808976384 | bytes 1311744 | tf_op jit(solution)/shard_map/dot_general | solution.py:39
  54.2 21.5 %all-gather.11.cloned.1.call-done = f32[2,1,1024,256]{2,3,1,0:T(8,128)} async-done(((f32[2,1,256,256]{2,3,1,0:T(8,128)}), f32[2,1,1024,256]{2,3,1,0:T(8,128)}) %all-gather.11.cloned.1.call-update) | async-done | bytes 2097168 | tf_op jit(solution)/shard_map/all_gather | solution.py:100
  75.7 6.3 %fusion.28 = f32[256,256]{1,0:T(8,128)S(1)} fusion(f32[2,1,1024,256]{2,3,1,0:T(8,128)} %all-gather.11.cloned.1.call-done, s32[256]{0:T(256)S(1)} %iota_add_fusion.1), kind=kOutput, calls=%fused_computation.60 | convolution fusion | flops 808976384 | bytes 1311744 | tf_op jit(solution)/shard_map/kh,phw->pkw/dot_general | solution.py:55
  82.0 4.9 %fusion.29 = f32[256,256]{1,0:T(8,128)S(1)} fusion(f32[2,1,1024,256]{2,3,1,0:T(8,128)S(1)} %copy-done.4, s32[256]{0:T(256)S(1)} %iota_add_fusion.1), kind=kOutput, calls=%fused_computation.61 | convolution fusion | flops 808976384 | bytes 1311744 | tf_op jit(solution)/shard_map/kh,phw->pkw/dot_general | solution.py:50
  86.9 5.3 %fusion.11 = f32[1,256,256]{1,2,0:T(8,128)S(1)} fusion(f32[256,256]{1,0:T(8,128)S(1)} %fusion.28, f32[2,1,1024,256]{2,3,1,0:T(8,128)S(1)} %copy-done.4, s32[256]{0:T(256)S(1)} %iota_add_fusion.1), kind=kOutput, calls=%fused_computation.28 | convolution fusion | flops 809041920 | bytes 1573888 | tf_op jit(solution)/shard_map/kh,phw->pkw/dot_general | solution.py:50
  92.2 4.9 %fusion.89 = (f32[1,1,256,256]{2,3,1,0:T(8,128)S(1)}, f32[1,1,256,256]{2,3,1,0:T(8,128)S(1)}) fusion(f32[1,256,256]{1,2,0:T(8,128)S(1)} %fusion.11, f32[1,1,256,256]{2,3,1,0:T(8,128)S(1)} %copy.10, f32[1,1,256,256]{2,3,1,0:T(8,128)S(1)} %copy.9, f32[256,256]{1,0:T(8,128)S(1)} %fusion.29, s32[256]{0:T(256)S(1)} %iota_add_fusion.1, ...), kind=kOutput, calls=%fused_computation.119 | convolution fusion | flops 809435136 | bytes 2622464 | tf_op jit(solution)/shard_map/kh,phw->pkw/dot_general | solution.py:55
  98.1 28.8 %all-reduce.2.cloned.1.call-done = f32[2,1,256,256]{2,3,1,0:T(8,128)} async-done(((f32[2,1,256,256]{2,3,1,0:T(8,128)}), f32[2,1,256,256]{2,3,1,0:T(8,128)}) %all-reduce.2.cloned.1.call-update) | async-done | bytes 524304 | tf_op jit(solution)/shard_map/psum | solution.py:122
  127.1 23.8 %all-gather.13.cloned.1.call-done = f32[2,1,1024,256]{2,3,1,0:T(8,128)} async-done(((f32[2,1,256,256]{2,3,1,0:T(8,128)}), f32[2,1,1024,256]{2,3,1,0:T(8,128)}) %all-gather.13.cloned.1.call-update) | async-done | bytes 2097168 | tf_op jit(solution)/shard_map/all_gather | solution.py:100
  150.9 6.3 %fusion.30 = f32[256,256]{1,0:T(8,128)S(1)} fusion(f32[2,1,1024,256]{2,3,1,0:T(8,128)} %all-gather.13.cloned.1.call-done, s32[256]{0:T(256)S(1)} %iota_add_fusion.1), kind=kOutput, calls=%fused_computation.62 | convolution fusion | flops 808976384 | bytes 1311744 | tf_op jit(solution)/shard_map/kh,phw->pkw/dot_general | solution.py:55
  157.2 4.9 %fusion.31 = f32[256,256]{1,0:T(8,128)S(1)} fusion(f32[2,1,1024,256]{2,3,1,0:T(8,128)S(1)} %copy-done.8, s32[256]{0:T(256)S(1)} %iota_add_fusion.1), kind=kOutput, calls=%fused_computation.63 | convolution fusion | flops 808976384 | bytes 1311744 | tf_op jit(solution)/shard_map/kh,phw->pkw/dot_general | solution.py:50
  162.1 5.1 %fusion.9 = f32[1,1,256,256]{2,3,1,0:T(8,128)S(1)} fusion(f32[256,256]{1,0:T(8,128)S(1)} %fusion.30, f32[2,1,1024,256]{2,3,1,0:T(8,128)S(1)} %copy-done.8, s32[256]{0:T(256)S(1)} %iota_add_fusion.1), kind=kOutput, calls=%fused_computation.24 | convolution fusion | flops 809041920 | bytes 1573888 | tf_op jit(solution)/shard_map/kh,phw->pkw/dot_general | solution.py:50
  167.2 4.9 %fusion.10 = f32[1,1,256,256]{2,3,1,0:T(8,128)S(1)} fusion(f32[256,256]{1,0:T(8,128)S(1)} %fusion.31, f32[2,1,1024,256]{2,3,1,0:T(8,128)S(1)} %copy-done.8, s32[256]{0:T(256)S(1)} %iota_add_fusion.1), kind=kOutput, calls=%fused_computation.26 | convolution fusion | flops 809041920 | bytes 1573888 | tf_op jit(solution)/shard_map/kh,phw->pkw/dot_general | solution.py:55
  173.5 45.3 %all-gather.15.cloned.1.call-done = f32[2,1,256,1024]{2,3,1,0:T(8,128)} async-done(((f32[2,1,256,256]{2,3,1,0:T(8,128)}), f32[2,1,256,1024]{2,3,1,0:T(8,128)}) %all-gather.15.cloned.1.call-update) | async-done | bytes 2097168 | tf_op jit(solution)/shard_map/all_gather | solution.py:81
  218.8 6.9 %fusion.19 = f32[256,256]{1,0:T(8,128)S(1)} fusion(f32[2,1,256,1024]{2,3,1,0:T(8,128)} %all-gather.15.cloned.1.call-done, s32[256]{0:T(256)S(1)} %iota_add_fusion), kind=kOutput, calls=%fused_computation.47 | convolution fusion | flops 808976384 | bytes 1311744 | tf_op jit(solution)/shard_map/dot_general | solution.py:39
  225.7 6.3 %fusion.8 = f32[256,256]{1,0:T(8,128)} fusion(f32[256,256]{1,0:T(8,128)S(1)} %copy-done.12, f32[256,256]{1,0:T(8,128)S(1)} %fusion.19, f32[2,1,256,1024]{2,3,1,0:T(8,128)S(1)} %copy-done.6, s32[256]{0:T(256)S(1)} %iota_add_fusion, pred[256]{0:T(512)(128)(4,1)S(1)} %get-tuple-element.14, pred[256]{0:T(512)(128)(4,1)S(1)} %get-tuple-element.15), kind=kOutput, calls=%fused_computation.22 | convolution fusion | flops 809304064 | bytes 1837056 | tf_op jit(solution)/shard_map/dot_general | solution.py:42
  232.2 26.7 %all-gather.25.cloned.1.call-done = f32[256,1024]{1,0:T(8,128)} async-done(((f32[256,256]{1,0:T(8,128)}), f32[256,1024]{1,0:T(8,128)}) %all-gather.25.cloned.1.call-update) | async-done | bytes 1048592 | tf_op jit(solution)/shard_map/all_gather | solution.py:81
  258.9 6.2 %convolution_bitcast_fusion = f32[1,1,256,256]{3,2,1,0:T(8,128)S(1)} fusion(f32[256,1024]{1,0:T(8,128)} %all-gather.25.cloned.1.call-done, s32[256]{0:T(256)S(1)} %iota_add_fusion), kind=kOutput, calls=%fused_computation.17 | convolution fusion | flops 808976384 | bytes 1311744 | tf_op jit(solution)/shard_map/dot_general | solution.py:42
  271.1 21.8 %all-gather.17.cloned.1.call-done = f32[2,1,1024,256]{3,2,1,0:T(8,128)} async-done(((f32[2,1,256,256]{3,2,1,0:T(8,128)}), f32[2,1,1024,256]{3,2,1,0:T(8,128)}) %all-gather.17.cloned.1.call-update) | async-done | bytes 2097168 | tf_op jit(solution)/shard_map/all_gather | solution.py:100
  292.9 6.9 %fusion.32 = f32[256,256]{1,0:T(8,128)S(1)} fusion(f32[2,1,1024,256]{3,2,1,0:T(8,128)} %all-gather.17.cloned.1.call-done, s32[256]{0:T(256)S(1)} %iota_add_fusion.1), kind=kOutput, calls=%fused_computation.64 | convolution fusion | flops 808976384 | bytes 1311744 | tf_op jit(solution)/shard_map/kh,phw->pkw/dot_general | solution.py:55
  299.9 5.6 %fusion.33 = f32[256,256]{1,0:T(8,128)S(1)} fusion(f32[2,1,1024,256]{3,2,1,0:T(8,128)S(1)} %copy-done.5, s32[256]{0:T(256)S(1)} %iota_add_fusion.1), kind=kOutput, calls=%fused_computation.65 | convolution fusion | flops 808976384 | bytes 1311744 | tf_op jit(solution)/shard_map/kh,phw->pkw/dot_general | solution.py:50
  305.4 6.0 %fusion.4 = f32[1,256,256]{1,2,0:T(8,128)S(1)} fusion(f32[256,256]{1,0:T(8,128)S(1)} %fusion.32, f32[2,1,1024,256]{3,2,1,0:T(8,128)S(1)} %copy-done.5, s32[256]{0:T(256)S(1)} %iota_add_fusion.1), kind=kOutput, calls=%fused_computation.14 | convolution fusion | flops 809041920 | bytes 1573888 | tf_op jit(solution)/shard_map/kh,phw->pkw/dot_general | solution.py:50
  311.4 5.6 %fusion.93 = (f32[1,1,256,256]{2,3,1,0:T(8,128)S(1)}, f32[1,1,256,256]{2,3,1,0:T(8,128)S(1)}) fusion(f32[1,256,256]{1,2,0:T(8,128)S(1)} %fusion.4, f32[1,1,256,256]{2,3,1,0:T(8,128)S(1)} %copy.10, f32[1,1,256,256]{2,3,1,0:T(8,128)S(1)} %copy.9, f32[256,256]{1,0:T(8,128)S(1)} %fusion.33, s32[256]{0:T(256)S(1)} %iota_add_fusion.1, ...), kind=kOutput, calls=%fused_computation.123 | convolution fusion | flops 809435136 | bytes 2622464 | tf_op jit(solution)/shard_map/kh,phw->pkw/dot_general | solution.py:55
  318.1 22.5 %all-gather.19.cloned.1.call-done = f32[2,1,1024,256]{2,3,1,0:T(8,128)} async-done(((f32[2,1,256,256]{2,3,1,0:T(8,128)}), f32[2,1,1024,256]{2,3,1,0:T(8,128)}) %all-gather.19.cloned.1.call-update) | async-done | bytes 2097168 | tf_op jit(solution)/shard_map/all_gather | solution.py:100
  340.6 6.3 %fusion.34 = f32[256,256]{1,0:T(8,128)S(1)} fusion(f32[2,1,1024,256]{2,3,1,0:T(8,128)} %all-gather.19.cloned.1.call-done, s32[256]{0:T(256)S(1)} %iota_add_fusion.1), kind=kOutput, calls=%fused_computation.66 | convolution fusion | flops 808976384 | bytes 1311744 | tf_op jit(solution)/shard_map/kh,phw->pkw/dot_general | solution.py:55
  346.9 4.9 %fusion.35 = f32[256,256]{1,0:T(8,128)S(1)} fusion(f32[2,1,1024,256]{2,3,1,0:T(8,128)S(1)} %copy-done.7, s32[256]{0:T(256)S(1)} %iota_add_fusion.1), kind=kOutput, calls=%fused_computation.67 | convolution fusion | flops 808976384 | bytes 1311744 | tf_op jit(solution)/shard_map/kh,phw->pkw/dot_general | solution.py:50
  351.8 5.1 %fusion.2 = f32[1,1,256,256]{2,3,1,0:T(8,128)S(1)} fusion(f32[256,256]{1,0:T(8,128)S(1)} %fusion.34, f32[2,1,1024,256]{2,3,1,0:T(8,128)S(1)} %copy-done.7, s32[256]{0:T(256)S(1)} %iota_add_fusion.1), kind=kOutput, calls=%fused_computation.10 | convolution fusion | flops 809041920 | bytes 1573888 | tf_op jit(solution)/shard_map/kh,phw->pkw/dot_general | solution.py:50
  356.9 4.9 %fusion.3 = f32[1,1,256,256]{2,3,1,0:T(8,128)S(1)} fusion(f32[256,256]{1,0:T(8,128)S(1)} %fusion.35, f32[2,1,1024,256]{2,3,1,0:T(8,128)S(1)} %copy-done.7, s32[256]{0:T(256)S(1)} %iota_add_fusion.1), kind=kOutput, calls=%fused_computation.12 | convolution fusion | flops 809041920 | bytes 1573888 | tf_op jit(solution)/shard_map/kh,phw->pkw/dot_general | solution.py:55
  362.7 45.8 %all-gather.21.cloned.1.call-done = f32[2,1,256,1024]{2,3,1,0:T(8,128)} async-done(((f32[2,1,256,256]{2,3,1,0:T(8,128)}), f32[2,1,256,1024]{2,3,1,0:T(8,128)}) %all-gather.21.cloned.1.call-update) | async-done | bytes 2097168 | tf_op jit(solution)/shard_map/all_gather | solution.py:81
  408.5 7.1 %fusion.18 = f32[256,256]{1,0:T(8,128)S(1)} fusion(f32[2,1,256,1024]{2,3,1,0:T(8,128)} %all-gather.21.cloned.1.call-done, s32[256]{0:T(256)S(1)} %iota_add_fusion), kind=kOutput, calls=%fused_computation.40 | convolution fusion | flops 808976384 | bytes 1311744 | tf_op jit(solution)/shard_map/dot_general | solution.py:39
  415.7 5.5 %fusion.13 = f32[1,256,256]{2,1,0:T(8,128)S(1)} fusion(f32[1,256,256]{2,1,0:T(8,128)S(1)} %copy-done.3, f32[256,256]{1,0:T(8,128)S(1)} %fusion.18, f32[2,1,256,1024]{2,3,1,0:T(8,128)S(1)} %copy-done.9, s32[256]{0:T(256)S(1)} %iota_add_fusion), kind=kOutput, calls=%fused_computation.33 | convolution fusion | flops 809172992 | bytes 1836032 | tf_op jit(solution)/shard_map/dot_general | solution.py:42
  (70 shorter events, 24.0 us)
Async XLA Ops:
  7.2 33.1 %all-gather.23.cloned.1.call-start = ((), (), s32[]{:S(2)}) async-start(), calls=%async_computation.7 | async-start | bytes 1310720 | tf_op jit(solution)/shard_map/all_gather | solution.py:81
  7.9 67.8 %all-gather.11.cloned.1.call-start = ((), (), s32[]{:S(2)}) async-start(), calls=%async_computation | async-start | bytes 2621440 | tf_op jit(solution)/shard_map/all_gather | solution.py:100
  40.3 6.9 %copy-start.10 = (f32[1,256,1024]{2,1,0:T(8,128)S(1)}, f32[1,256,1024]{2,1,0:T(8,128)}, u32[]{:S(2)}) copy-start(f32[1,256,1024]{2,1,0:T(8,128)} %all-gather.23.cloned.1.call-done) | copy-start | bytes 3145732
  47.2 6.7 %copy-start.2 = (f32[2,1,256,256]{3,2,1,0:T(8,128)S(1)}, f32[2,1,256,256]{3,2,1,0:T(8,128)}, u32[]{:S(2)}) copy-start(f32[2,1,256,256]{3,2,1,0:T(8,128)} %param.5) | copy-start | bytes 1572868
  53.6 73.2 %all-reduce.2.cloned.1.call-start = ((), (), s32[]{:S(2)}) async-start(), calls=%async_computation.1 | async-start | bytes 1048576 | tf_op jit(solution)/shard_map/psum | solution.py:122
  75.7 6.3 %copy-start.4 = (f32[2,1,1024,256]{2,3,1,0:T(8,128)S(1)}, f32[2,1,1024,256]{2,3,1,0:T(8,128)}, u32[]{:S(2)}) copy-start(f32[2,1,1024,256]{2,3,1,0:T(8,128)} %all-gather.11.cloned.1.call-done) | copy-start | bytes 6291460
  98.0 52.8 %all-gather.13.cloned.1.call-start = ((), (), s32[]{:S(2)}) async-start(), calls=%async_computation.2 | async-start | bytes 2621440 | tf_op jit(solution)/shard_map/all_gather | solution.py:100
  126.9 91.9 %all-gather.15.cloned.1.call-start = ((), (), s32[]{:S(2)}) async-start(), calls=%async_computation.3 | async-start | bytes 2621440 | tf_op jit(solution)/shard_map/all_gather | solution.py:81
  150.9 6.3 %copy-start.8 = (f32[2,1,1024,256]{2,3,1,0:T(8,128)S(1)}, f32[2,1,1024,256]{2,3,1,0:T(8,128)}, u32[]{:S(2)}) copy-start(f32[2,1,1024,256]{2,3,1,0:T(8,128)} %all-gather.13.cloned.1.call-done) | copy-start | bytes 6291460
  173.0 85.9 %all-gather.25.cloned.1.call-start = ((), (), s32[]{:S(2)}) async-start(), calls=%async_computation.8 | async-start | bytes 1310720 | tf_op jit(solution)/shard_map/all_gather | solution.py:81
  173.4 52.2 %copy-start.12 = (f32[256,256]{1,0:T(8,128)S(1)}, f32[256,256]{1,0:T(8,128)}, u32[]{:S(2)}) copy-start(f32[256,256]{1,0:T(8,128)} %param.6) | copy-start | bytes 786436
  218.8 6.9 %copy-start.6 = (f32[2,1,256,1024]{2,3,1,0:T(8,128)S(1)}, f32[2,1,256,1024]{2,3,1,0:T(8,128)}, u32[]{:S(2)}) copy-start(f32[2,1,256,1024]{2,3,1,0:T(8,128)} %all-gather.15.cloned.1.call-done) | copy-start | bytes 6291460
  232.0 60.9 %all-gather.17.cloned.1.call-start = ((), (), s32[]{:S(2)}) async-start(), calls=%async_computation.4 | async-start | bytes 2621440 | tf_op jit(solution)/shard_map/all_gather | solution.py:100
  258.9 6.2 %copy-start.11 = (f32[256,1024]{1,0:T(8,128)S(1)}, f32[256,1024]{1,0:T(8,128)}, u32[]{:S(2)}) copy-start(f32[256,1024]{1,0:T(8,128)} %all-gather.25.cloned.1.call-done) | copy-start | bytes 3145732
  270.8 69.7 %all-gather.19.cloned.1.call-start = ((), (), s32[]{:S(2)}) async-start(), calls=%async_computation.5 | async-start | bytes 2621440 | tf_op jit(solution)/shard_map/all_gather | solution.py:100
  292.9 7.0 %copy-start.5 = (f32[2,1,1024,256]{3,2,1,0:T(8,128)S(1)}, f32[2,1,1024,256]{3,2,1,0:T(8,128)}, u32[]{:S(2)}) copy-start(f32[2,1,1024,256]{3,2,1,0:T(8,128)} %all-gather.17.cloned.1.call-done) | copy-start | bytes 6291460
  317.9 90.6 %all-gather.21.cloned.1.call-start = ((), (), s32[]{:S(2)}) async-start(), calls=%async_computation.6 | async-start | bytes 2621440 | tf_op jit(solution)/shard_map/all_gather | solution.py:81
  340.6 6.3 %copy-start.7 = (f32[2,1,1024,256]{2,3,1,0:T(8,128)S(1)}, f32[2,1,1024,256]{2,3,1,0:T(8,128)}, u32[]{:S(2)}) copy-start(f32[2,1,1024,256]{2,3,1,0:T(8,128)} %all-gather.19.cloned.1.call-done) | copy-start | bytes 6291460
  362.7 53.0 %copy-start.3 = (f32[1,256,256]{2,1,0:T(8,128)S(1)}, f32[1,256,256]{2,1,0:T(8,128)}, u32[]{:S(2)}) copy-start(f32[1,256,256]{2,1,0:T(8,128)} %param.4) | copy-start | bytes 786436
  408.5 7.1 %copy-start.9 = (f32[2,1,256,1024]{2,3,1,0:T(8,128)S(1)}, f32[2,1,256,1024]{2,3,1,0:T(8,128)}, u32[]{:S(2)}) copy-start(f32[2,1,256,1024]{2,3,1,0:T(8,128)} %all-gather.21.cloned.1.call-done) | copy-start | bytes 6291460
  421.2 11.4 %copy-start = (f32[1,256,256]{2,1,0:T(8,128)}, f32[1,256,256]{2,1,0:T(8,128)S(1)}, u32[]{:S(2)}) copy-start(f32[1,256,256]{2,1,0:T(8,128)S(1)} %fusion.13) | copy-start | bytes 786436
  421.2 10.1 %copy-start.1 = (f32[3,1,256,256]{3,2,1,0:T(8,128)S(1)}, f32[3,1,256,256]{3,2,1,0:T(8,128)}, u32[]{:S(2)}) copy-start(f32[3,1,256,256]{3,2,1,0:T(8,128)} %param.7) | copy-start | bytes 2359300
  421.2 9.9 %collective-permute-start = (f32[1,256,256]{2,1,0:T(8,128)S(1)}, f32[1,256,256]{2,1,0:T(8,128)S(1)}, u32[]{:S(2)}, u32[]{:S(2)}) collective-permute-start(f32[1,256,256]{2,1,0:T(8,128)S(1)} %fusion.13), channel_id=1, source_target_pairs={{16,0},{17,1},{18,2},{19,3},{20,4},{21,5},{22,6},{23,7},{24,8},{25... | collective-permute-start | bytes 786440 | tf_op jit(solution)/shard_map/ppermute | solution.py:15
  422.7 7.0 %collective-permute-start.2 = (f32[1,256,1]{2,1,0:T(8,128)S(1)}, f32[1,256,1]{2,1,0:T(8,128)S(1)}, u32[]{:S(2)}, u32[]{:S(2)}) collective-permute-start(f32[1,256,1]{2,1,0:T(8,128)S(1)} %slice.95), channel_id=1, source_target_pairs={{1,0},{2,1},{3,2},{5,4},{6,5},{7,6},{9,8},{10,9},{11,10},{13,12},{... | collective-permute-start | bytes 3080 | tf_op jit(solution)/shard_map/ppermute | solution.py:15
  424.0 5.7 %collective-permute-start.1 = (f32[1,1,256]{2,1,0:T(1,128)S(1)}, f32[1,1,256]{2,1,0:T(1,128)S(1)}, u32[]{:S(2)}, u32[]{:S(2)}) collective-permute-start(f32[1,1,256]{2,1,0:T(1,128)S(1)} %slice.93), channel_id=1, source_target_pairs={{4,0},{8,4},{12,8},{5,1},{9,5},{13,9},{6,2},{10,6},{14,10},{7,3},{... | collective-permute-start | bytes 3080 | tf_op jit(solution)/shard_map/ppermute | solution.py:15
Sparse Core Ops, SparseCore 0:
  9.5 30.6 all-gather.22
  53.8 21.9 all-gather.10
  98.2 28.6 all-reduce.1
  128.3 22.5 all-gather.12
  173.1 45.6 all-gather.14
  232.1 26.7 all-gather.24
  270.9 21.9 all-gather.16
  318.0 22.5 all-gather.18
  362.8 45.6 all-gather.20
where the time goes:
time: 448 us; the launch traced here: 440 us
  waiting for transfers between devices  275 us (61%)
  matrix products  137 us (31%)
  between operations  14.7 us (3%)
  other arithmetic  6.46 us (1%)
  starting transfers between devices  5.72 us (1%)
    all_gather x4, waiting for transfers between devices, along_columns(): lax.all_gather(field, 'col', axis=3, tiled=True)  150 us
    all_gather x4, waiting for transfers between devices, along_rows(): lax.all_gather(field, 'row', axis=2, tiled=True)  89.6 us
    dot_general x8, matrix products, apply_sin(): jnp.einsum('kh,phw->pkw', sine_part, part, precision=highest, preferred_e...  46.2 us
    dot_general x8, matrix products, apply_cos(): jnp.einsum('kh,phw->pkw', cosines, part, precision=highest, preferred_ele...  41.7 us
    psum x1, waiting for transfers between devices, shards(): summed_image = lax.psum(local_sum, 'depth')  28.8 us
    dot_general x4, matrix products, apply_sin(): jnp.dot(part, sine_part, precision=highest, preferred_element_type=jnp.fl...  24.9 us
    dot_general x4, matrix products, apply_cos(): jnp.dot(part, cosines, precision=highest, preferred_element_type=jnp.floa...  24.4 us
  transfers between devices with their start and end apart: 12, of which 11 were waited for; matrix products, arithmetic and copies ran while one was open for 0% of the time, Pallas kernels for 0%

commit v1 on v0

--- a/solution.py
+++ b/solution.py
@@ -7,6 +7,14 @@
 step_size = 1.0
 shrink_level = 0.5
 highest = lax.Precision.HIGHEST
+
+
+def tiled_gather(shard, axis, dim):
+    size = lax.axis_size(axis)
+    repeats = [size if d == dim else 1 for d in range(shard.ndim)]
+    return lax.all_to_all(
+        jnp.tile(shard, repeats), axis, split_axis=dim, concat_axis=dim, tiled=True
+    )
 
 
 def shifted(array, axis, by):
@@ -96,10 +104,7 @@
         return left_mult(cosines, sine_part, portion, keep)
 
     start_value = jnp.zeros((parts_out,) + field.shape[1:], jnp.float32)
-    result = (
-        accumulate(start_value, lax.all_gather(field, "row", axis=2, tiled=True), jnp.int32(0))
-        * factor
-    )
+    result = accumulate(start_value, tiled_gather(field, "row", 2), jnp.int32(0)) * factor
     return result
 
 

time: 448 us -> 481 us (1.074)
  blocking collectives: 0 us -> 84.5 us
  waiting for transfers between devices: 275 us -> 207 us
  local copies, waits for them, and re-layouts: 0.51 us -> 12.8 us
    all_gather x4 -> x0, waiting for transfers between devices: 89.6 us -> none  [along_rows(): lax.all_gather(field, 'row', axis=2, tiled=True)]
    all_to_all x0 -> x3, blocking collectives: none -> 84.5 us  [tiled_gather(): lax.all_to_all(jnp.tile(shard, repeats), axis, split_axis=dim, concat_axi...]
    all_to_all x0 -> x1, waiting for transfers between devices: none -> 25.2 us  [tiled_gather(): lax.all_to_all(jnp.tile(shard, repeats), axis, split_axis=dim, concat_axi...]
    slice x0 -> x4, local copies, waits for them, and re-layouts: none -> 6.47 us  [complex_mix(): real_part = apply_cos(field[0]) - apply_sin(field[1])]
  transfers between devices with their start and end apart: 12 -> 9, of which waited for: 11 -> 8; matrix products, arithmetic and copies ran while one was open for 0% -> 0% of each run, Pallas kernels for 0% -> 0%
where the time goes in v1:
time: 481 us; the launch traced here: 472 us
  waiting for transfers between devices  207 us (43%)
  matrix products  141 us (29%)
  blocking collectives  84.5 us (18%)
  between operations  14.7 us (3%)
  local copies, waits for them, and re-layouts  12.8 us (3%)
  starting transfers between devices  8.16 us (2%)
    all_gather x4, waiting for transfers between devices, along_columns(): lax.all_gather(field, 'col', axis=3, tiled=True)  148 us
    all_to_all x3, blocking collectives, tiled_gather(): lax.all_to_all(jnp.tile(shard, repeats), axis, split_axis=dim, concat_axi...  84.5 us
    dot_general x8, matrix products, apply_sin(): jnp.einsum('kh,phw->pkw', sine_part, part, precision=highest, preferred_e...  46.3 us
    dot_general x8, matrix products, apply_cos(): jnp.einsum('kh,phw->pkw', cosines, part, precision=highest, preferred_ele...  45.8 us
    psum x1, waiting for transfers between devices, shards(): summed_image = lax.psum(local_sum, 'depth')  27.2 us
    dot_general x4, matrix products, apply_cos(): jnp.dot(part, cosines, precision=highest, preferred_element_type=jnp.floa...  25.5 us
    all_to_all x1, waiting for transfers between devices, tiled_gather(): lax.all_to_all(jnp.tile(shard, repeats), axis, split_axis=dim, concat_axi...  25.2 us
    dot_general x4, matrix products, apply_sin(): jnp.dot(part, sine_part, precision=highest, preferred_element_type=jnp.fl...  23.6 us
  transfers between devices with their start and end apart: 9, of which 8 were waited for; matrix products, arithmetic and copies ran while one was open for 0% of the time, Pallas kernels for 0%

profile of v1, /device:TPU:0, one launch (start us, length us, event | category | flops | bytes accessed | tf_op | source)
XLA Modules:
  0.0 472.4 jit_solution(15797672033838252894)
XLA Ops:
  7.9 32.4 %all-gather.11.cloned.1.call-done = f32[1,256,1024]{2,1,0:T(8,128)} async-done(((f32[1,256,256]{2,1,0:T(8,128)}), f32[1,256,1024]{2,1,0:T(8,128)}) %all-gather.11.cloned.1.call-update) | async-done | bytes 1048592 | tf_op jit(solution)/shard_map/all_gather | solution.py:89
  40.3 6.9 %convolution_bitcast_fusion.2 = f32[1,1,256,256]{2,3,1,0:T(8,128)S(1)} fusion(f32[1,256,1024]{2,1,0:T(8,128)} %all-gather.11.cloned.1.call-done, s32[256]{0:T(256)S(1)} %iota_add_fusion), kind=kOutput, calls=%fused_computation.31 | convolution fusion | flops 808976384 | bytes 1311744 | tf_op jit(solution)/shard_map/dot_general | solution.py:50
  47.2 5.6 %convolution_bitcast_fusion.3 = f32[1,1,256,256]{2,3,1,0:T(8,128)S(1)} fusion(f32[1,256,1024]{2,1,0:T(8,128)S(1)} %copy-done.6, s32[256]{0:T(256)S(1)} %iota_add_fusion), kind=kOutput, calls=%fused_computation.32 | convolution fusion | flops 808976384 | bytes 1311744 | tf_op jit(solution)/shard_map/dot_general | solution.py:47
  59.3 25.2 %all-to-all-done = f32[2,1,1024,256]{3,0,1,2:T(2,128)S(1)} async-done(((f32[2,1,1024,256]{3,0,1,2:T(2,128)}), f32[2,1,1024,256]{3,0,1,2:T(2,128)S(1)}, u32[]{:S(2)}, u32[]{:S(2)}) %all-to-all-start) | async-done | bytes 2097184 | tf_op jit(solution)/shard_map/all_to_all | solution.py:15
  86.1 5.6 %fusion.40 = f32[256,256]{1,0:T(8,128)S(1)} fusion(f32[1,1,1024,256]{3,0,1,2:T(1,128)S(1)} %get-tuple-element.12, s32[256]{0:T(256)S(1)} %iota_add_fusion.1), kind=kOutput, calls=%fused_computation.64 | convolution fusion | flops 808976384 | bytes 1311744 | tf_op jit(solution)/shard_map/kh,phw->pkw/dot_general | solution.py:63
  91.8 6.0 %fusion.42 = f32[256,256]{1,0:T(8,128)S(1)} fusion(f32[1,1,1024,256]{3,0,1,2:T(1,128)S(1)} %get-tuple-element.12, s32[256]{0:T(256)S(1)} %iota_add_fusion.1), kind=kOutput, calls=%fused_computation.66 | convolution fusion | flops 808976384 | bytes 1311744 | tf_op jit(solution)/shard_map/kh,phw->pkw/dot_general | solution.py:58
  97.8 5.6 %fusion.11 = f32[1,256,256]{1,2,0:T(8,128)S(1)} fusion(f32[256,256]{1,0:T(8,128)S(1)} %fusion.40, f32[1,1,1024,256]{3,0,1,2:T(1,128)S(1)} %get-tuple-element.11, s32[256]{0:T(256)S(1)} %iota_add_fusion.1), kind=kOutput, calls=%fused_computation.28 | convolution fusion | flops 809041920 | bytes 1573888 | tf_op jit(solution)/shard_map/kh,phw->pkw/dot_general | solution.py:58
  103.4 5.8 %fusion.121 = (f32[1,1,256,256]{2,3,1,0:T(8,128)S(1)}, f32[1,1,256,256]{2,3,1,0:T(8,128)S(1)}) fusion(f32[1,256,256]{1,2,0:T(8,128)S(1)} %fusion.11, f32[1,1,256,256]{2,3,1,0:T(8,128)S(1)} %copy.27, f32[1,1,256,256]{2,3,1,0:T(8,128)S(1)} %copy.26, f32[256,256]{1,0:T(8,128)S(1)} %fusion.42, s32[256]{0:T(256)S(1)} %iota_add_fusion.1, ...), kind=kOutput, calls=%fused_computation.143 | convolution fusion | flops 809435136 | bytes 2622464 | tf_op jit(solution)/shard_map/kh,phw->pkw/dot_general | solution.py:63
  110.2 27.2 %all-reduce.2.cloned.1.call-done = f32[2,256,256]{1,2,0:T(8,128)} async-done(((f32[2,256,256]{1,2,0:T(8,128)}), f32[2,256,256]{1,2,0:T(8,128)}) %all-reduce.2.cloned.1.call-update) | async-done | bytes 524304 | tf_op jit(solution)/shard_map/psum | solution.py:127
  139.2 28.2 %all_to_all.20 = f32[2,1,1024,256]{3,0,1,2:T(2,128)S(1)} all-to-all(f32[2,1,1024,256]{3,0,1,2:T(2,128)S(1)} %bitcast.183), channel_id=1, replica_groups=mesh['depth'=2,'row'=4,'col'=4] {'row'}, dimensions={2} | all-to-all | bytes 4194304 | tf_op jit(solution)/shard_map/all_to_all | solution.py:15
  169.0 5.6 %fusion.36 = f32[256,256]{1,0:T(8,128)S(1)} fusion(f32[1,1,1024,256]{3,0,1,2:T(1,128)S(1)} %get-tuple-element.10, s32[256]{0:T(256)S(1)} %iota_add_fusion.1), kind=kOutput, calls=%fused_computation.60 | convolution fusion | flops 808976384 | bytes 1311744 | tf_op jit(solution)/shard_map/kh,phw->pkw/dot_general | solution.py:58
  174.7 6.0 %fusion.34 = f32[256,256]{1,0:T(8,128)S(1)} fusion(f32[1,1,1024,256]{3,0,1,2:T(1,128)S(1)} %get-tuple-element.10, s32[256]{0:T(256)S(1)} %iota_add_fusion.1), kind=kOutput, calls=%fused_computation.58 | convolution fusion | flops 808976384 | bytes 1311744 | tf_op jit(solution)/shard_map/kh,phw->pkw/dot_general | solution.py:63
  180.7 5.6 %fusion.10 = f32[1,1,256,256]{2,3,1,0:T(8,128)S(1)} fusion(f32[256,256]{1,0:T(8,128)S(1)} %fusion.36, f32[1,1,1024,256]{3,0,1,2:T(1,128)S(1)} %get-tuple-element.9, s32[256]{0:T(256)S(1)} %iota_add_fusion.1), kind=kOutput, calls=%fused_computation.26 | convolution fusion | flops 809041920 | bytes 1573888 | tf_op jit(solution)/shard_map/kh,phw->pkw/dot_general | solution.py:63
  186.4 5.8 %fusion.9 = f32[1,1,256,256]{2,3,1,0:T(8,128)S(1)} fusion(f32[256,256]{1,0:T(8,128)S(1)} %fusion.34, f32[1,1,1024,256]{3,0,1,2:T(1,128)S(1)} %get-tuple-element.9, s32[256]{0:T(256)S(1)} %iota_add_fusion.1), kind=kOutput, calls=%fused_computation.24 | convolution fusion | flops 809041920 | bytes 1573888 | tf_op jit(solution)/shard_map/kh,phw->pkw/dot_general | solution.py:58
  193.1 44.8 %all-gather.7.cloned.1.call-done = f32[2,1,256,1024]{2,3,1,0:T(8,128)} async-done(((f32[2,1,256,256]{2,3,1,0:T(8,128)}), f32[2,1,256,1024]{2,3,1,0:T(8,128)}) %all-gather.7.cloned.1.call-update) | async-done | bytes 2097168 | tf_op jit(solution)/shard_map/all_gather | solution.py:89
  237.9 6.9 %fusion.19 = f32[256,256]{1,0:T(8,128)S(1)} fusion(f32[2,1,256,1024]{2,3,1,0:T(8,128)} %all-gather.7.cloned.1.call-done, s32[256]{0:T(256)S(1)} %iota_add_fusion), kind=kOutput, calls=%fused_computation.43 | convolution fusion | flops 808976384 | bytes 1311744 | tf_op jit(solution)/shard_map/dot_general | solution.py:47
  244.8 6.3 %fusion.8 = f32[256,256]{1,0:T(8,128)} fusion(f32[256,256]{1,0:T(8,128)S(1)} %copy-done.8, f32[256,256]{1,0:T(8,128)S(1)} %fusion.19, f32[2,1,256,1024]{2,3,1,0:T(8,128)S(1)} %copy-done.4, s32[256]{0:T(256)S(1)} %iota_add_fusion, pred[256]{0:T(512)(128)(4,1)S(1)} %get-tuple-element.22, pred[256]{0:T(512)(128)(4,1)S(1)} %get-tuple-element.23), kind=kOutput, calls=%fused_computation.22 | convolution fusion | flops 809304064 | bytes 1837056 | tf_op jit(solution)/shard_map/dot_general | solution.py:50
  251.4 26.7 %all-gather.13.cloned.1.call-done = f32[256,1024]{1,0:T(8,128)} async-done(((f32[256,256]{1,0:T(8,128)}), f32[256,1024]{1,0:T(8,128)}) %all-gather.13.cloned.1.call-update) | async-done | bytes 1048592 | tf_op jit(solution)/shard_map/all_gather | solution.py:89
  278.0 6.1 %convolution_bitcast_fusion.1 = f32[1,1,256,256]{3,2,1,0:T(8,128)S(1)} fusion(f32[256,1024]{1,0:T(8,128)} %all-gather.13.cloned.1.call-done, s32[256]{0:T(256)S(1)} %iota_add_fusion), kind=kOutput, calls=%fused_computation.18 | convolution fusion | flops 808976384 | bytes 1311744 | tf_op jit(solution)/shard_map/dot_general | solution.py:47
  290.1 28.2 %all_to_all.21 = f32[2,1,1024,256]{3,0,1,2:T(2,128)S(1)} all-to-all(f32[2,1,1024,256]{3,0,1,2:T(2,128)S(1)} %bitcast.184), channel_id=1, replica_groups=mesh['depth'=2,'row'=4,'col'=4] {'row'}, dimensions={2} | all-to-all | bytes 4194304 | tf_op jit(solution)/shard_map/all_to_all | solution.py:15
  319.9 5.6 %fusion.28 = f32[256,256]{1,0:T(8,128)S(1)} fusion(f32[1,1,1024,256]{3,0,1,2:T(1,128)S(1)} %get-tuple-element.8, s32[256]{0:T(256)S(1)} %iota_add_fusion.1), kind=kOutput, calls=%fused_computation.52 | convolution fusion | flops 808976384 | bytes 1311744 | tf_op jit(solution)/shard_map/kh,phw->pkw/dot_general | solution.py:63
  325.6 5.8 %fusion.30 = f32[256,256]{1,0:T(8,128)S(1)} fusion(f32[1,1,1024,256]{3,0,1,2:T(1,128)S(1)} %get-tuple-element.8, s32[256]{0:T(256)S(1)} %iota_add_fusion.1), kind=kOutput, calls=%fused_computation.54 | convolution fusion | flops 808976384 | bytes 1311744 | tf_op jit(solution)/shard_map/kh,phw->pkw/dot_general | solution.py:58
  331.3 5.6 %fusion.4 = f32[1,256,256]{1,2,0:T(8,128)S(1)} fusion(f32[256,256]{1,0:T(8,128)S(1)} %fusion.28, f32[1,1,1024,256]{3,0,1,2:T(1,128)S(1)} %get-tuple-element.7, s32[256]{0:T(256)S(1)} %iota_add_fusion.1), kind=kOutput, calls=%fused_computation.14 | convolution fusion | flops 809041920 | bytes 1573888 | tf_op jit(solution)/shard_map/kh,phw->pkw/dot_general | solution.py:58
  337.0 6.1 %fusion.125 = (f32[1,1,256,256]{2,3,1,0:T(8,128)S(1)}, f32[1,1,256,256]{2,3,1,0:T(8,128)S(1)}) fusion(f32[1,256,256]{1,2,0:T(8,128)S(1)} %fusion.4, f32[1,1,256,256]{2,3,1,0:T(8,128)S(1)} %copy.27, f32[1,1,256,256]{2,3,1,0:T(8,128)S(1)} %copy.26, f32[256,256]{1,0:T(8,128)S(1)} %fusion.30, s32[256]{0:T(256)S(1)} %iota_add_fusion.1, ...), kind=kOutput, calls=%fused_computation.147 | convolution fusion | flops 809435136 | bytes 2622464 | tf_op jit(solution)/shard_map/kh,phw->pkw/dot_general | solution.py:63
  343.9 28.1 %all_to_all.22 = f32[2,1,1024,256]{3,0,1,2:T(2,128)S(1)} all-to-all(f32[2,1,1024,256]{3,0,1,2:T(2,128)S(1)} %bitcast.185), channel_id=1, replica_groups=mesh['depth'=2,'row'=4,'col'=4] {'row'}, dimensions={2} | all-to-all | bytes 4194304 | tf_op jit(solution)/shard_map/all_to_all | solution.py:15
  373.6 5.6 %fusion.24 = f32[256,256]{1,0:T(8,128)S(1)} fusion(f32[1,1,1024,256]{3,0,1,2:T(1,128)S(1)} %get-tuple-element.6, s32[256]{0:T(256)S(1)} %iota_add_fusion.1), kind=kOutput, calls=%fused_computation.48 | convolution fusion | flops 808976384 | bytes 1311744 | tf_op jit(solution)/shard_map/kh,phw->pkw/dot_general | solution.py:58
  379.2 5.8 %fusion.22 = f32[256,256]{1,0:T(8,128)S(1)} fusion(f32[1,1,1024,256]{3,0,1,2:T(1,128)S(1)} %get-tuple-element.6, s32[256]{0:T(256)S(1)} %iota_add_fusion.1), kind=kOutput, calls=%fused_computation.46 | convolution fusion | flops 808976384 | bytes 1311744 | tf_op jit(solution)/shard_map/kh,phw->pkw/dot_general | solution.py:63
  385.1 5.6 %fusion.3 = f32[1,1,256,256]{2,3,1,0:T(8,128)S(1)} fusion(f32[256,256]{1,0:T(8,128)S(1)} %fusion.24, f32[1,1,1024,256]{3,0,1,2:T(1,128)S(1)} %get-tuple-element.5, s32[256]{0:T(256)S(1)} %iota_add_fusion.1), kind=kOutput, calls=%fused_computation.12 | convolution fusion | flops 809041920 | bytes 1573888 | tf_op jit(solution)/shard_map/kh,phw->pkw/dot_general | solution.py:63
  390.7 5.8 %fusion.2 = f32[1,1,256,256]{2,3,1,0:T(8,128)S(1)} fusion(f32[256,256]{1,0:T(8,128)S(1)} %fusion.22, f32[1,1,1024,256]{3,0,1,2:T(1,128)S(1)} %get-tuple-element.5, s32[256]{0:T(256)S(1)} %iota_add_fusion.1), kind=kOutput, calls=%fused_computation.10 | convolution fusion | flops 809041920 | bytes 1573888 | tf_op jit(solution)/shard_map/kh,phw->pkw/dot_general | solution.py:58
  397.4 44.3 %all-gather.9.cloned.1.call-done = f32[2,1,256,1024]{2,3,1,0:T(8,128)} async-done(((f32[2,1,256,256]{2,3,1,0:T(8,128)}), f32[2,1,256,1024]{2,3,1,0:T(8,128)}) %all-gather.9.cloned.1.call-update) | async-done | bytes 2097168 | tf_op jit(solution)/shard_map/all_gather | solution.py:89
  441.7 6.9 %fusion.18 = f32[256,256]{1,0:T(8,128)S(1)} fusion(f32[2,1,256,1024]{2,3,1,0:T(8,128)} %all-gather.9.cloned.1.call-done, s32[256]{0:T(256)S(1)} %iota_add_fusion), kind=kOutput, calls=%fused_computation.40 | convolution fusion | flops 808976384 | bytes 1311744 | tf_op jit(solution)/shard_map/dot_general | solution.py:47
  448.6 5.5 %fusion.13 = f32[1,256,256]{2,1,0:T(8,128)S(1)} fusion(f32[1,256,256]{2,1,0:T(8,128)S(1)} %copy-done.3, f32[256,256]{1,0:T(8,128)S(1)} %fusion.18, f32[2,1,256,1024]{2,3,1,0:T(8,128)S(1)} %copy-done.5, s32[256]{0:T(256)S(1)} %iota_add_fusion), kind=kOutput, calls=%fused_computation.33 | convolution fusion | flops 809172992 | bytes 1836032 | tf_op jit(solution)/shard_map/dot_general | solution.py:50
  (67 shorter events, 36.3 us)
Async XLA Ops:
  7.2 33.1 %all-gather.11.cloned.1.call-start = ((), (), s32[]{:S(2)}) async-start(), calls=%async_computation.7 | async-start | bytes 1310720 | tf_op jit(solution)/shard_map/all_gather | solution.py:89
  40.3 6.9 %copy-start.6 = (f32[1,256,1024]{2,1,0:T(8,128)S(1)}, f32[1,256,1024]{2,1,0:T(8,128)}, u32[]{:S(2)}) copy-start(f32[1,256,1024]{2,1,0:T(8,128)} %all-gather.11.cloned.1.call-done) | copy-start | bytes 3145732
  55.1 3.8 copy-start.2
  55.1 29.4 %all-to-all-start = ((f32[2,1,1024,256]{3,0,1,2:T(2,128)}), f32[2,1,1024,256]{3,0,1,2:T(2,128)S(1)}, u32[]{:S(2)}, u32[]{:S(2)}) async-start(f32[2,1,1024,256]{3,0,1,2:T(2,128)} %bitcast.7), calls=%async_computation | async-start | bytes 4194304 | tf_op jit(solution)/shard_map/all_to_all | solution.py:15
  58.9 78.5 %all-reduce.2.cloned.1.call-start = ((), (), s32[]{:S(2)}) async-start(), calls=%async_computation.4 | async-start | bytes 1048576 | tf_op jit(solution)/shard_map/psum | solution.py:127
  110.1 127.8 %all-gather.7.cloned.1.call-start = ((), (), s32[]{:S(2)}) async-start(), calls=%async_computation.5 | async-start | bytes 2621440 | tf_op jit(solution)/shard_map/all_gather | solution.py:89
  193.0 85.0 %all-gather.13.cloned.1.call-start = ((), (), s32[]{:S(2)}) async-start(), calls=%async_computation.8 | async-start | bytes 1310720 | tf_op jit(solution)/shard_map/all_gather | solution.py:89
  193.1 51.7 %copy-start.8 = (f32[256,256]{1,0:T(8,128)S(1)}, f32[256,256]{1,0:T(8,128)}, u32[]{:S(2)}) copy-start(f32[256,256]{1,0:T(8,128)} %param.6) | copy-start | bytes 786436
  237.9 6.9 %copy-start.4 = (f32[2,1,256,1024]{2,3,1,0:T(8,128)S(1)}, f32[2,1,256,1024]{2,3,1,0:T(8,128)}, u32[]{:S(2)}) copy-start(f32[2,1,256,1024]{2,3,1,0:T(8,128)} %all-gather.7.cloned.1.call-done) | copy-start | bytes 6291460
  251.1 190.6 %all-gather.9.cloned.1.call-start = ((), (), s32[]{:S(2)}) async-start(), calls=%async_computation.6 | async-start | bytes 2621440 | tf_op jit(solution)/shard_map/all_gather | solution.py:89
  278.0 6.2 %copy-start.7 = (f32[256,1024]{1,0:T(8,128)S(1)}, f32[256,1024]{1,0:T(8,128)}, u32[]{:S(2)}) copy-start(f32[256,1024]{1,0:T(8,128)} %all-gather.13.cloned.1.call-done) | copy-start | bytes 3145732
  397.4 51.2 %copy-start.3 = (f32[1,256,256]{2,1,0:T(8,128)S(1)}, f32[1,256,256]{2,1,0:T(8,128)}, u32[]{:S(2)}) copy-start(f32[1,256,256]{2,1,0:T(8,128)} %param.4) | copy-start | bytes 786436
  441.7 6.9 %copy-start.5 = (f32[2,1,256,1024]{2,3,1,0:T(8,128)S(1)}, f32[2,1,256,1024]{2,3,1,0:T(8,128)}, u32[]{:S(2)}) copy-start(f32[2,1,256,1024]{2,3,1,0:T(8,128)} %all-gather.9.cloned.1.call-done) | copy-start | bytes 6291460
  454.1 11.4 %copy-start = (f32[1,256,256]{2,1,0:T(8,128)}, f32[1,256,256]{2,1,0:T(8,128)S(1)}, u32[]{:S(2)}) copy-start(f32[1,256,256]{2,1,0:T(8,128)S(1)} %fusion.13) | copy-start | bytes 786436
  454.1 10.1 %copy-start.1 = (f32[3,1,256,256]{3,2,1,0:T(8,128)S(1)}, f32[3,1,256,256]{3,2,1,0:T(8,128)}, u32[]{:S(2)}) copy-start(f32[3,1,256,256]{3,2,1,0:T(8,128)} %param.7) | copy-start | bytes 2359300
  454.1 9.9 %collective-permute-start = (f32[1,256,256]{2,1,0:T(8,128)S(1)}, f32[1,256,256]{2,1,0:T(8,128)S(1)}, u32[]{:S(2)}, u32[]{:S(2)}) collective-permute-start(f32[1,256,256]{2,1,0:T(8,128)S(1)} %fusion.13), channel_id=1, source_target_pairs={{16,0},{17,1},{18,2},{19,3},{20,4},{21,5},{22,6},{23,7},{24,8},{25... | collective-permute-start | bytes 786440 | tf_op jit(solution)/shard_map/ppermute | solution.py:23
  455.6 7.0 %collective-permute-start.2 = (f32[1,256,1]{2,1,0:T(8,128)S(1)}, f32[1,256,1]{2,1,0:T(8,128)S(1)}, u32[]{:S(2)}, u32[]{:S(2)}) collective-permute-start(f32[1,256,1]{2,1,0:T(8,128)S(1)} %slice.95), channel_id=1, source_target_pairs={{1,0},{2,1},{3,2},{5,4},{6,5},{7,6},{9,8},{10,9},{11,10},{13,12},{... | collective-permute-start | bytes 3080 | tf_op jit(solution)/shard_map/ppermute | solution.py:23
  456.9 5.7 %collective-permute-start.1 = (f32[1,1,256]{2,1,0:T(1,128)S(1)}, f32[1,1,256]{2,1,0:T(1,128)S(1)}, u32[]{:S(2)}, u32[]{:S(2)}) collective-permute-start(f32[1,1,256]{2,1,0:T(1,128)S(1)} %slice.93), channel_id=1, source_target_pairs={{4,0},{8,4},{12,8},{5,1},{9,5},{13,9},{6,2},{10,6},{14,10},{7,3},{... | collective-permute-start | bytes 3080 | tf_op jit(solution)/shard_map/ppermute | solution.py:23
Sparse Core Ops, SparseCore 0:
  9.5 30.6 all-gather.10
  110.2 27.1 all-reduce.1
  193.1 44.7 all-gather.6
  251.2 26.7 all-gather.12
  397.5 44.1 all-gather.8
